TPU v7x, 256 devices: a whole 4x4x8 slice. The times are simulated.
256 devices in a mesh: row: 4 (over y), col: 16 (over z, core), layer: 4 (over x).
Axes of the slice: x: 4, y: 4, z: 8, core: 2. Of those that a mesh axis runs over, the one named last changes fastest.
Arguments:
- blocks: bfloat16 [5632, 128, 128], P(('col', 'layer')), may hold values from -6 to 6
- block_aux: int32 [5632], P(('col', 'layer')), may hold values from 0 to 23
- block_row: int32 [5632], P(('col', 'layer')), may hold values from 0 to 15, as said below
- block_col: int32 [5632], P(('col', 'layer')), may hold values from 0 to 159, as said below
- extents: int32 [5632], P(('col', 'layer')), may hold values from 32 to 128
- occ_green: bfloat16 [20480, 2048], P('layer', 'row'), may hold values from -0.00390625 to 0.00390625
- virt_green: bfloat16 [20480, 2048], P('layer', 'row'), may hold values from -0.00390625 to 0.00390625
Outputs:
- chi: float32 [24, 24], replicated
Inputs may be any that keep to these rules, and one draw needn't show every extreme that they name: block_row[n] numbers the block of 128 window functions that tile n covers. The owner of tile n is the pair (block_row[n], block_col[n] // 40). Within each device's share of 88 consecutive entries no owner appears more than 2 times, and one owner, the same for every share, appears exactly 2 times in every share.
All inputs are finite; a program needn't handle non-finite values.
Results may differ from a plain program's by a relative error of at most 0.0003.
Values may be sent and summed in bfloat16 or wider, within the bound.
No kernel may reach another device: no remote copies, remote signals or barrier semaphores. Data moves between devices by JAX's collectives and lax.ppermute only.
A program may use at most 192 MiB of HBM per device.

v0:
```python
import jax
import jax.numpy as jnp
from jax import lax
from jax.sharding import PartitionSpec as P

NP = 24


def on_device(blocks, block_aux, block_row, block_col, extents, occ_green, virt_green):
    row_count = lax.axis_size("row")
    col_count = lax.axis_size("col")
    layer_count = lax.axis_size("layer")
    held_count = blocks.shape[0]
    tile_side = blocks.shape[1]
    aux_count = NP
    owner_count = col_count * layer_count
    capacity = max(2, held_count // owner_count + 1)
    layer_blocks = occ_green.shape[0] // tile_side
    columns = jnp.arange(tile_side, dtype=jnp.int32)
    masked_tiles = jnp.where(
        columns[None, None, :] < extents[:, None, None], blocks, jnp.zeros((), blocks.dtype)
    )
    layer_of = block_col // layer_blocks
    target = block_row * layer_count + layer_of
    kept_col = block_col - layer_of * layer_blocks
    marked = (target[:, None] == jnp.arange(owner_count, dtype=jnp.int32)[None, :]).astype(
        jnp.int32
    )
    earlier = jnp.cumsum(marked, axis=0) - marked
    placed = target * capacity + jnp.sum(earlier * marked, axis=1)
    send_tiles = (
        jnp.zeros((owner_count * capacity, tile_side, tile_side), blocks.dtype)
        .at[placed]
        .set(masked_tiles)
    )
    send_meta = (
        jnp.zeros((owner_count * capacity, 2), jnp.int32)
        .at[placed]
        .set(jnp.stack([block_aux, kept_col], axis=1))
    )
    send_tiles = send_tiles.reshape(col_count, layer_count, capacity, tile_side, tile_side)
    send_meta = send_meta.reshape(col_count, layer_count, capacity, 2)
    total_slots = col_count * layer_count * capacity
    got_tiles, got_meta = (
        lax.all_to_all(
            send_tiles.reshape(total_slots, tile_side, tile_side),
            ("col", "layer"),
            split_axis=0,
            concat_axis=0,
            tiled=True,
        ),
        lax.all_to_all(
            send_meta.reshape(total_slots, 2),
            ("col", "layer"),
            split_axis=0,
            concat_axis=0,
            tiled=True,
        ),
    )
    group_size = col_count * capacity
    got_tiles = got_tiles.reshape(layer_count, group_size, tile_side, tile_side)
    got_meta = got_meta.reshape(layer_count, group_size, 2)
    occ_cols, virt_cols = (occ_green, virt_green)
    width_here = occ_cols.shape[1]
    offsets = jnp.arange(tile_side, dtype=jnp.int32)

    def add_group(totals, record):
        occ_total, virt_total = totals
        tile_group, meta_group = record
        row_index = meta_group[:, 1][:, None] * tile_side + offsets[None, :]
        occ_rows = occ_cols[row_index]
        virt_rows = virt_cols[row_index]
        occ_term = jnp.einsum(
            "gsv,gls->gvl", occ_rows, tile_group, preferred_element_type=jnp.float32
        )
        virt_term = jnp.einsum(
            "gvs,gsl->gvl", tile_group, virt_rows, preferred_element_type=jnp.float32
        )
        aux_index = meta_group[:, 0]
        return (
            (occ_total.at[aux_index].add(occ_term), virt_total.at[aux_index].add(virt_term)),
            None,
        )

    start_totals = (
        jnp.zeros((aux_count, width_here, tile_side), jnp.float32),
        jnp.zeros((aux_count, tile_side, width_here), jnp.float32),
    )
    (occ_total, virt_total), _ = lax.scan(add_group, start_totals, (got_tiles, got_meta))
    occ_done, virt_done = (
        lax.psum_scatter(occ_total, "layer", scatter_dimension=1, tiled=True),
        lax.psum_scatter(virt_total, "layer", scatter_dimension=2, tiled=True),
    )
    mesh_count = row_count * layer_count
    thin_rows = tile_side // mesh_count
    stack_count = mesh_count // col_count
    narrow = occ_done.shape[1]
    occ_five = occ_done.reshape(aux_count, 1, col_count, thin_rows, tile_side)
    virt_five = virt_done.reshape(aux_count, stack_count, col_count, thin_rows, narrow)
    occ_moved, virt_moved = (
        lax.all_to_all(occ_five, "col", split_axis=2, concat_axis=1, tiled=True),
        lax.all_to_all(virt_five, "col", split_axis=2, concat_axis=1, tiled=True),
    )
    virt_four = virt_moved.reshape(aux_count, mesh_count, thin_rows, narrow)
    virt_back = lax.all_to_all(virt_four, ("row", "layer"), split_axis=1, concat_axis=3, tiled=True)
    occ_final = occ_moved.reshape(aux_count, col_count, thin_rows, tile_side)
    virt_final = virt_back.reshape(aux_count, thin_rows, col_count, tile_side)
    chi_part = jnp.einsum(
        "pcji,qjci->pq",
        occ_final,
        virt_final,
        precision=lax.Precision.HIGHEST,
        preferred_element_type=jnp.float32,
    )
    return lax.psum(chi_part, ("row", "col", "layer"))


def solution(mesh):
    in_specs = (
        P(("col", "layer"), None, None),
        P(("col", "layer")),
        P(("col", "layer")),
        P(("col", "layer")),
        P(("col", "layer")),
        P("layer", "row"),
        P("layer", "row"),
    )
    out_specs = P()
    return jax.shard_map(
        on_device, mesh=mesh, in_specs=in_specs, out_specs=out_specs, check_vma=False
    )
```

profile of v0, /device:TPU:1, one launch (start us, length us, event | category | flops | bytes accessed | tf_op | source)
XLA Modules:
  0.0 813.1 jit_solution(16769600088540931036)
XLA Ops:
  6.5 0.7 subtract_bitcast_fusion
  7.2 0.7 multiply_add_fusion
  7.9 0.1 fusion.21
  8.0 0.1 reduce_window_sum.11
  8.1 0.2 select_reduce_fusion
  8.3 0.7 pad_add_fusion
  8.9 0.1 copy.18
  9.0 0.8 scatter_custom_fusion.2
  9.9 1.1 copy.19
  11.0 13.0 %all-to-all-start = ((s32[64,2,2]{1,2,0:T(2,128)}), s32[64,2,2]{1,2,0:T(2,128)S(1)}, u32[]{:S(2)}, u32[]{:S(2)}) async-start(s32[64,2,2]{1,2,0:T(2,128)} %copy.19), calls=%async_computation | async-start | bytes 131072 | tf_op jit(solution)/shard_map/all_to_all | solution.py:52
  24.0 0.7 iota_compare_fusion
  24.7 2.1 broadcast_select_fusion
  26.8 3.0 broadcast_in_dim.41
  29.7 12.7 %scatter_fusion.2 = bf16[128,128,128]{2,1,0:T(8,128)(2,1)} fusion(bf16[128,128,128]{2,1,0:T(8,128)(2,1)} %broadcast_in_dim.41, s32[88]{0:T(128)S(1)} %compare_select_fusion.2, bf16[88,128,128]{2,1,0:T(8,128)(2,1)S(1)} %broadcast_select_fusion), kind=kCustom, calls=%fused_computation.5 | custom fusion | bytes 8651104 | tf_op jit(solution)/shard_map/scatter | solution.py:34
  42.4 0.0 all-to-all-done
  42.4 10.4 %all-to-all-start.1 = ((bf16[128,128,128]{2,1,0:T(8,128)(2,1)}), bf16[128,128,128]{2,1,0:T(8,128)(2,1)}, u32[]{:S(2)}, u32[]{:S(2)}) async-start(bf16[128,128,128]{2,1,0:T(8,128)(2,1)} %scatter_fusion.2), calls=%async_computation.1 | async-start | bytes 8388608 | tf_op jit(solution)/shard_map/all_to_all | solution.py:45
  52.9 0.0 reduce-scatter.5.cloned.1.call-start
  52.9 0.1 reshape.109
  53.0 93.4 %all-to-all-done.1 = bf16[128,128,128]{2,1,0:T(8,128)(2,1)} async-done(((bf16[128,128,128]{2,1,0:T(8,128)(2,1)}), bf16[128,128,128]{2,1,0:T(8,128)(2,1)}, u32[]{:S(2)}, u32[]{:S(2)}) %all-to-all-start.1) | async-done | bytes 4194336 | tf_op jit(solution)/shard_map/all_to_all | solution.py:45
  146.4 3.4 broadcast_in_dim.22
  149.8 3.4 broadcast_in_dim.38
  153.2 366.1 %while.13 = (s32[]{:T(128)}, f32[24,512,128]{2,1,0:T(8,128)}, f32[24,128,512]{2,1,0:T(8,128)}, s32[4,32,2]{1,0,2:T(4,128)S(1)}, bf16[5120,512]{1,0:T(8,128)(2,1)...) while((s32[]{:T(128)}, f32[24,512,128]{2,1,0:T(8,128)}, ...), condition=%wide.region_7.8_spmd.clone, body=%wide.region_4.7_spmd.clone.sunk | while | flops 1077956736 | bytes 94423512 | solution.py:89
  153.2 0.1 fusion.37
  153.3 20.6 %gather_fusion.1 = bf16[4096,512]{1,0:T(8,128)(2,1)} fusion(bf16[5120,512]{1,0:T(8,128)(2,1)} %get-tuple-element.167, s32[4096]{0:T(1024)S(1)} %fusion.37), kind=kCustom, calls=%fused_computation.1.clone.clone.1 | custom fusion | bytes 8404992 | tf_op jit(solution)/shard_map/while/body/eval_jaxpr/gather | solution.py:72
  173.8 7.0 fusion.39
  180.8 18.0 %scatter_fusion.1 = f32[24,128,512]{2,1,0:T(8,128)} fusion(f32[24,128,512]{2,1,0:T(8,128)} %get-tuple-element.155, s32[32]{0:T(128)S(1)} %get-tuple-element.143, f32[32,128,512]{2,1,0:T(8,128)} %fusion.39), kind=kCustom, calls=%fused_computation.3.clone.clone.1 | custom fusion | flops 2097152 | bytes 25165952 | tf_op jit(solution)/shard_map/while/body/eval_jaxpr/scatter-add | solution.py:81
  198.8 20.6 %gather_fusion = bf16[4096,512]{1,0:T(8,128)(2,1)} fusion(bf16[5120,512]{1,0:T(8,128)(2,1)} %get-tuple-element.165, s32[4096]{0:T(1024)S(1)} %fusion.37), kind=kCustom, calls=%fused_computation.clone.clone.1 | custom fusion | bytes 8404992 | tf_op jit(solution)/shard_map/while/body/eval_jaxpr/gather | solution.py:71
  219.3 7.0 fusion.38
  226.4 17.8 %scatter_fusion = f32[24,512,128]{2,1,0:T(8,128)} fusion(f32[24,512,128]{2,1,0:T(8,128)} %get-tuple-element.154, s32[32]{0:T(128)S(1)} %get-tuple-element.143, f32[32,512,128]{2,1,0:T(8,128)} %fusion.38), kind=kCustom, calls=%fused_computation.2.clone.clone.1 | custom fusion | flops 2097152 | bytes 25165952 | tf_op jit(solution)/shard_map/while/body/eval_jaxpr/scatter-add | solution.py:81
  244.2 0.1 fusion.37
  244.3 20.6 %gather_fusion.1 = bf16[4096,512]{1,0:T(8,128)(2,1)} fusion(bf16[5120,512]{1,0:T(8,128)(2,1)} %get-tuple-element.167, s32[4096]{0:T(1024)S(1)} %fusion.37), kind=kCustom, calls=%fused_computation.1.clone.clone.1 | custom fusion | bytes 8404992 | tf_op jit(solution)/shard_map/while/body/eval_jaxpr/gather | solution.py:72
  264.9 7.0 fusion.39
  271.8 18.1 %scatter_fusion.1 = f32[24,128,512]{2,1,0:T(8,128)} fusion(f32[24,128,512]{2,1,0:T(8,128)} %get-tuple-element.155, s32[32]{0:T(128)S(1)} %get-tuple-element.143, f32[32,128,512]{2,1,0:T(8,128)} %fusion.39), kind=kCustom, calls=%fused_computation.3.clone.clone.1 | custom fusion | flops 2097152 | bytes 25165952 | tf_op jit(solution)/shard_map/while/body/eval_jaxpr/scatter-add | solution.py:81
  289.9 20.6 %gather_fusion = bf16[4096,512]{1,0:T(8,128)(2,1)} fusion(bf16[5120,512]{1,0:T(8,128)(2,1)} %get-tuple-element.165, s32[4096]{0:T(1024)S(1)} %fusion.37), kind=kCustom, calls=%fused_computation.clone.clone.1 | custom fusion | bytes 8404992 | tf_op jit(solution)/shard_map/while/body/eval_jaxpr/gather | solution.py:71
  310.5 7.0 fusion.38
  317.5 18.1 %scatter_fusion = f32[24,512,128]{2,1,0:T(8,128)} fusion(f32[24,512,128]{2,1,0:T(8,128)} %get-tuple-element.154, s32[32]{0:T(128)S(1)} %get-tuple-element.143, f32[32,512,128]{2,1,0:T(8,128)} %fusion.38), kind=kCustom, calls=%fused_computation.2.clone.clone.1 | custom fusion | flops 2097152 | bytes 25165952 | tf_op jit(solution)/shard_map/while/body/eval_jaxpr/scatter-add | solution.py:81
  335.6 0.1 fusion.37
  335.7 20.6 %gather_fusion.1 = bf16[4096,512]{1,0:T(8,128)(2,1)} fusion(bf16[5120,512]{1,0:T(8,128)(2,1)} %get-tuple-element.167, s32[4096]{0:T(1024)S(1)} %fusion.37), kind=kCustom, calls=%fused_computation.1.clone.clone.1 | custom fusion | bytes 8404992 | tf_op jit(solution)/shard_map/while/body/eval_jaxpr/gather | solution.py:72
  356.3 7.0 fusion.39
  363.3 18.5 %scatter_fusion.1 = f32[24,128,512]{2,1,0:T(8,128)} fusion(f32[24,128,512]{2,1,0:T(8,128)} %get-tuple-element.155, s32[32]{0:T(128)S(1)} %get-tuple-element.143, f32[32,128,512]{2,1,0:T(8,128)} %fusion.39), kind=kCustom, calls=%fused_computation.3.clone.clone.1 | custom fusion | flops 2097152 | bytes 25165952 | tf_op jit(solution)/shard_map/while/body/eval_jaxpr/scatter-add | solution.py:81
  381.7 20.6 %gather_fusion = bf16[4096,512]{1,0:T(8,128)(2,1)} fusion(bf16[5120,512]{1,0:T(8,128)(2,1)} %get-tuple-element.165, s32[4096]{0:T(1024)S(1)} %fusion.37), kind=kCustom, calls=%fused_computation.clone.clone.1 | custom fusion | bytes 8404992 | tf_op jit(solution)/shard_map/while/body/eval_jaxpr/gather | solution.py:71
  402.3 7.0 fusion.38
  409.3 18.4 %scatter_fusion = f32[24,512,128]{2,1,0:T(8,128)} fusion(f32[24,512,128]{2,1,0:T(8,128)} %get-tuple-element.154, s32[32]{0:T(128)S(1)} %get-tuple-element.143, f32[32,512,128]{2,1,0:T(8,128)} %fusion.38), kind=kCustom, calls=%fused_computation.2.clone.clone.1 | custom fusion | flops 2097152 | bytes 25165952 | tf_op jit(solution)/shard_map/while/body/eval_jaxpr/scatter-add | solution.py:81
  427.7 0.1 fusion.37
  427.8 20.6 %gather_fusion.1 = bf16[4096,512]{1,0:T(8,128)(2,1)} fusion(bf16[5120,512]{1,0:T(8,128)(2,1)} %get-tuple-element.167, s32[4096]{0:T(1024)S(1)} %fusion.37), kind=kCustom, calls=%fused_computation.1.clone.clone.1 | custom fusion | bytes 8404992 | tf_op jit(solution)/shard_map/while/body/eval_jaxpr/gather | solution.py:72
  448.4 7.0 fusion.39
  455.4 18.1 %scatter_fusion.1 = f32[24,128,512]{2,1,0:T(8,128)} fusion(f32[24,128,512]{2,1,0:T(8,128)} %get-tuple-element.155, s32[32]{0:T(128)S(1)} %get-tuple-element.143, f32[32,128,512]{2,1,0:T(8,128)} %fusion.39), kind=kCustom, calls=%fused_computation.3.clone.clone.1 | custom fusion | flops 2097152 | bytes 25165952 | tf_op jit(solution)/shard_map/while/body/eval_jaxpr/scatter-add | solution.py:81
  473.5 20.6 %gather_fusion = bf16[4096,512]{1,0:T(8,128)(2,1)} fusion(bf16[5120,512]{1,0:T(8,128)(2,1)} %get-tuple-element.165, s32[4096]{0:T(1024)S(1)} %fusion.37), kind=kCustom, calls=%fused_computation.clone.clone.1 | custom fusion | bytes 8404992 | tf_op jit(solution)/shard_map/while/body/eval_jaxpr/gather | solution.py:71
  494.1 7.0 fusion.38
  501.1 18.2 %scatter_fusion = f32[24,512,128]{2,1,0:T(8,128)} fusion(f32[24,512,128]{2,1,0:T(8,128)} %get-tuple-element.154, s32[32]{0:T(128)S(1)} %get-tuple-element.143, f32[32,512,128]{2,1,0:T(8,128)} %fusion.38), kind=kCustom, calls=%fused_computation.2.clone.clone.1 | custom fusion | flops 2097152 | bytes 25165952 | tf_op jit(solution)/shard_map/while/body/eval_jaxpr/scatter-add | solution.py:81
  519.2 0.0 reduce-scatter.5.cloned.1.call-update
  519.3 0.2 reduce-scatter.3.cloned.1.call-start
  519.5 0.5 reduce-scatter.3.cloned.1.call-update
  520.0 66.1 %reduce-scatter.5.cloned.1.call-done = f32[24,128,128]{2,1,0:T(8,128)} async-done(((f32[24,128,512]{2,1,0:T(8,128)}), f32[24,128,128]{2,1,0:T(8,128)}) %reduce-scatter.5.cloned.1.call-update) | async-done | bytes 1572880 | tf_op jit(solution)/shard_map/reduce_scatter | solution.py:92
  586.1 3.5 copy.23
  589.6 7.7 all-to-all-start.3
  597.2 57.7 %reduce-scatter.3.cloned.1.call-done = f32[24,128,128]{2,1,0:T(8,128)} async-done(((f32[24,512,128]{2,1,0:T(8,128)}), f32[24,128,128]{2,1,0:T(8,128)}) %reduce-scatter.3.cloned.1.call-update) | async-done | bytes 1572880 | tf_op jit(solution)/shard_map/reduce_scatter | solution.py:91
  654.9 2.3 copy.22
  657.3 0.0 all-to-all-done.3
  657.3 47.2 %all_to_all.47 = f32[24,1,16,8,128]{4,0,3,1,2:T(8,128)S(1)} all-to-all(f32[24,1,16,8,128]{4,0,3,1,2:T(8,128)S(1)} %bitcast.69), channel_id=1, replica_groups=mesh['row'=4,'col'=16,'layer'=4] {'col'}, dimensions={2} | all-to-all | bytes 3145728 | tf_op jit(solution)/shard_map/all_to_all | solution.py:101
  704.5 27.5 %all_to_all.48 = f32[24,16,8,128]{3,0,2,1:T(8,128)S(1)} all-to-all(f32[24,16,8,128]{3,0,2,1:T(8,128)S(1)} %bitcast.68), channel_id=1, replica_groups=mesh['row'=4,'col'=16,'layer'=4] {'row','layer'}, dimensions={1} | all-to-all | bytes 3145728 | tf_op jit(solution)/shard_map/all_to_all | solution.py:105
  732.0 1.6 fusion.16
  733.5 72.8 %psum.7 = f32[24,24]{1,0:T(8,128)} all-reduce(f32[24,24]{1,0:T(8,128)S(1)} %fusion.16), channel_id=1, replica_groups=mesh['row'=4,'col'=16,'layer'=4] {'row','col','layer'}, use_global_device_ids=true, to_apply=%region_10.11 | all-reduce | flops 576 | bytes 4608 | tf_op jit(solution)/shard_map/psum | solution.py:115
  (10 shorter events, 0.1 us)
Async XLA Ops:
  11.0 31.5 %all-to-all-start = ((s32[64,2,2]{1,2,0:T(2,128)}), s32[64,2,2]{1,2,0:T(2,128)S(1)}, u32[]{:S(2)}, u32[]{:S(2)}) async-start(s32[64,2,2]{1,2,0:T(2,128)} %copy.19), calls=%async_computation | async-start | bytes 131072 | tf_op jit(solution)/shard_map/all_to_all | solution.py:52
  42.4 103.9 %all-to-all-start.1 = ((bf16[128,128,128]{2,1,0:T(8,128)(2,1)}), bf16[128,128,128]{2,1,0:T(8,128)(2,1)}, u32[]{:S(2)}, u32[]{:S(2)}) async-start(bf16[128,128,128]{2,1,0:T(8,128)(2,1)} %scatter_fusion.2), calls=%async_computation.1 | async-start | bytes 8388608 | tf_op jit(solution)/shard_map/all_to_all | solution.py:45
  52.9 533.3 %reduce-scatter.5.cloned.1.call-start = ((), (), s32[]{:S(2)}) async-start(), calls=%async_computation.8 | async-start | bytes 7864320 | tf_op jit(solution)/shard_map/reduce_scatter | solution.py:92
  519.3 135.7 %reduce-scatter.3.cloned.1.call-start = ((), (), s32[]{:S(2)}) async-start(), calls=%async_computation.7 | async-start | bytes 7864320 | tf_op jit(solution)/shard_map/reduce_scatter | solution.py:91
  589.6 67.7 %all-to-all-start.3 = ((f32[24,1,16,8,128]{4,0,3,1,2:T(8,128)}), f32[24,1,16,8,128]{4,0,3,1,2:T(8,128)S(1)}, u32[]{:S(2)}, u32[]{:S(2)}) async-start(f32[24,1,16,8,128]{4,0,3,1,2:T(8,128)} %bitcast.6), calls=%async_computation.5 | async-start | bytes 3145728 | tf_op jit(solution)/shard_map/all_to_all | solution.py:102
Sparse Core Ops, SparseCore 0:
  519.4 66.6 reduce-scatter.4
  588.7 66.2 reduce-scatter.2
where the time goes:
time: 815 us; the launch traced here: 813 us
  waiting for transfers between devices  218 us (27%)
  local copies, waits for them, and re-layouts  195 us (24%)
  other arithmetic  151 us (19%)
  blocking collectives  147 us (18%)
  matrix products  57.5 us (7%)
  starting transfers between devices  31.3 us (4%)
  between operations  13.5 us (2%)
    all_to_all x1, waiting for transfers between devices, on_device(): lax.all_to_all(send_tiles.reshape(total_slots, tile_side, tile_side), ('c...  93.4 us
    gather x4, local copies, waits for them, and re-layouts, add_group(): virt_rows = virt_cols[row_index]  82.3 us
    gather x4, local copies, waits for them, and re-layouts, add_group(): occ_rows = occ_cols[row_index]  82.3 us
    psum x1, blocking collectives, on_device(): return lax.psum(chi_part, ('row', 'col', 'layer'))  72.8 us
    scatter-add x4, other arithmetic, add_group(): virt_total.at[aux_index].add(virt_term)  72.6 us
    scatter-add x4, other arithmetic, add_group(): occ_total.at[aux_index].add(occ_term)  72.5 us
    reduce_scatter x1, waiting for transfers between devices, on_device(): lax.psum_scatter(virt_total, 'layer', scatter_dimension=2, tiled=True)  66.1 us
    reduce_scatter x1, waiting for transfers between devices, on_device(): lax.psum_scatter(occ_total, 'layer', scatter_dimension=1, tiled=True)  57.7 us
  transfers between devices with their start and end apart: 5, of which 3 were waited for; matrix products, arithmetic and copies ran while one was open for 3% of the time, Pallas kernels for 0%

commit v1 on v0

--- a/solution.py
+++ b/solution.py
@@ -4,6 +4,22 @@
 from jax.sharding import PartitionSpec as P
 
 NP = 24
+
+
+def swapped_with_each(value, axis, split, join):
+    ways, here = (lax.axis_size(axis), lax.axis_index(axis))
+    width = value.shape[split] // ways
+    dims = list(value.shape)
+    dims[split] = width
+    height = dims[join]
+    dims[join] = height * ways
+    full = jnp.zeros(dims, value.dtype)
+    for mask in range(ways):
+        part = lax.dynamic_slice_in_dim(value, (here ^ mask) * width, width, axis=split)
+        if mask:
+            part = lax.ppermute(part, axis, [(d, d ^ mask) for d in range(ways)])
+        full = lax.dynamic_update_slice_in_dim(full, part, (here ^ mask) * height, axis=join)
+    return full
 
 
 def on_device(blocks, block_aux, block_row, block_col, extents, occ_green, virt_green):
@@ -102,7 +118,7 @@
         lax.all_to_all(virt_five, "col", split_axis=2, concat_axis=1, tiled=True),
     )
     virt_four = virt_moved.reshape(aux_count, mesh_count, thin_rows, narrow)
-    virt_back = lax.all_to_all(virt_four, ("row", "layer"), split_axis=1, concat_axis=3, tiled=True)
+    virt_back = swapped_with_each(virt_four, ("row", "layer"), 1, 3)
     occ_final = occ_moved.reshape(aux_count, col_count, thin_rows, tile_side)
     virt_final = virt_back.reshape(aux_count, thin_rows, col_count, tile_side)
     chi_part = jnp.einsum(

time: 815 us -> 792 us (0.972)
  blocking collectives: 147 us -> 75.4 us
  starting transfers between devices: 31.3 us -> 67.2 us
  waiting for transfers between devices: 218 us -> 227 us
    all_to_all x2 -> x0, blocking collectives: 74.7 us -> none  [the longest x1 47.2 us: on_device(): lax.all_to_all(occ_five, 'col', split_axis=2, concat_axis=1, tiled=True)]
    ppermute x0 -> x15, starting transfers between devices: none -> 28.2 us  [swapped_with_each(): part = lax.ppermute(part, axis, [(d, d ^ mask) for d in range(ways)])]
  transfers between devices with their start and end apart: 5 -> 21, of which waited for: 3 -> 6; matrix products, arithmetic and copies ran while one was open for 3% -> 3% of each run, Pallas kernels for 0% -> 0%
where the time goes in v1:
time: 792 us; the launch traced here: 790 us
  waiting for transfers between devices  227 us (29%)
  local copies, waits for them, and re-layouts  197 us (25%)
  other arithmetic  151 us (19%)
  blocking collectives  75.4 us (10%)
  starting transfers between devices  67.2 us (8%)
  matrix products  58.5 us (7%)
  between operations  13.7 us (2%)
    all_to_all x1, waiting for transfers between devices, on_device(): lax.all_to_all(send_tiles.reshape(total_slots, tile_side, tile_side), ('c...  93.4 us
    gather x4, local copies, waits for them, and re-layouts, add_group(): virt_rows = virt_cols[row_index]  82.6 us
    gather x4, local copies, waits for them, and re-layouts, add_group(): occ_rows = occ_cols[row_index]  82.6 us
    psum x1, blocking collectives, on_device(): return lax.psum(chi_part, ('row', 'col', 'layer'))  75.4 us
    scatter-add x4, other arithmetic, add_group(): virt_total.at[aux_index].add(virt_term)  72.9 us
    scatter-add x4, other arithmetic, add_group(): occ_total.at[aux_index].add(occ_term)  72.5 us
    reduce_scatter x1, waiting for transfers between devices, on_device(): lax.psum_scatter(virt_total, 'layer', scatter_dimension=2, tiled=True)  65.9 us
    reduce_scatter x1, waiting for transfers between devices, on_device(): lax.psum_scatter(occ_total, 'layer', scatter_dimension=1, tiled=True)  58.3 us
  transfers between devices with their start and end apart: 21, of which 6 were waited for; matrix products, arithmetic and copies ran while one was open for 3% of the time, Pallas kernels for 0%

profile of v1, /device:TPU:1, one launch (start us, length us, event | category | flops | bytes accessed | tf_op | source)
XLA Modules:
  0.0 790.0 jit_solution(3229699630187155139)
XLA Ops:
  6.5 0.7 subtract_bitcast_fusion
  7.2 0.7 multiply_add_fusion
  8.1 0.2 select_reduce_fusion
  8.3 0.7 pad_add_fusion
  9.0 0.8 scatter_custom_fusion.2
  9.9 1.1 copy.25
  11.0 13.0 %all-to-all-start = ((s32[64,2,2]{1,2,0:T(2,128)}), s32[64,2,2]{1,2,0:T(2,128)S(1)}, u32[]{:S(2)}, u32[]{:S(2)}) async-start(s32[64,2,2]{1,2,0:T(2,128)} %copy.25), calls=%async_computation | async-start | bytes 131072 | tf_op jit(solution)/shard_map/all_to_all | solution.py:68
  23.9 0.7 iota_compare_fusion
  24.7 2.1 broadcast_select_fusion
  26.7 3.0 broadcast_in_dim.44
  29.7 12.8 %scatter_fusion.2 = bf16[128,128,128]{2,1,0:T(8,128)(2,1)} fusion(bf16[128,128,128]{2,1,0:T(8,128)(2,1)} %broadcast_in_dim.44, s32[88]{0:T(128)S(1)} %compare_select_fusion.2, bf16[88,128,128]{2,1,0:T(8,128)(2,1)S(1)} %broadcast_select_fusion), kind=kCustom, calls=%fused_computation.5 | custom fusion | bytes 8651104 | tf_op jit(solution)/shard_map/scatter | solution.py:50
  42.5 10.4 %all-to-all-start.1 = ((bf16[128,128,128]{2,1,0:T(8,128)(2,1)}), bf16[128,128,128]{2,1,0:T(8,128)(2,1)}, u32[]{:S(2)}, u32[]{:S(2)}) async-start(bf16[128,128,128]{2,1,0:T(8,128)(2,1)} %scatter_fusion.2), calls=%async_computation.1 | async-start | bytes 8388608 | tf_op jit(solution)/shard_map/all_to_all | solution.py:61
  53.1 93.4 %all-to-all-done.1 = bf16[128,128,128]{2,1,0:T(8,128)(2,1)} async-done(((bf16[128,128,128]{2,1,0:T(8,128)(2,1)}), bf16[128,128,128]{2,1,0:T(8,128)(2,1)}, u32[]{:S(2)}, u32[]{:S(2)}) %all-to-all-start.1) | async-done | bytes 4194336 | tf_op jit(solution)/shard_map/all_to_all | solution.py:61
  146.5 3.4 broadcast_in_dim.40
  149.9 3.4 broadcast_in_dim.41
  153.2 367.0 %while.13 = (s32[]{:T(128)}, f32[24,512,128]{2,1,0:T(8,128)}, f32[24,128,512]{2,1,0:T(8,128)}, s32[4,32,2]{1,0,2:T(4,128)S(1)}, bf16[5120,512]{1,0:T(8,128)(2,1)...) while((s32[]{:T(128)}, f32[24,512,128]{2,1,0:T(8,128)}, ...), condition=%wide.region_7.8_spmd.clone, body=%wide.region_4.7_spmd.clone.sunk | while | flops 1077956736 | bytes 94423512 | solution.py:105
  153.3 20.6 %gather_fusion.1 = bf16[4096,512]{1,0:T(8,128)(2,1)} fusion(bf16[5120,512]{1,0:T(8,128)(2,1)} %get-tuple-element.189, s32[4096]{0:T(1024)S(1)} %fusion.37), kind=kCustom, calls=%fused_computation.1.clone.clone.1 | custom fusion | bytes 8404992 | tf_op jit(solution)/shard_map/while/body/eval_jaxpr/gather | solution.py:88
  174.0 7.0 fusion.39
  181.0 18.1 %scatter_fusion.1 = f32[24,128,512]{2,1,0:T(8,128)} fusion(f32[24,128,512]{2,1,0:T(8,128)} %get-tuple-element.177, s32[32]{0:T(128)S(1)} %get-tuple-element.165, f32[32,128,512]{2,1,0:T(8,128)} %fusion.39), kind=kCustom, calls=%fused_computation.3.clone.clone.1 | custom fusion | flops 2097152 | bytes 25165952 | tf_op jit(solution)/shard_map/while/body/eval_jaxpr/scatter-add | solution.py:97
  199.0 20.6 %gather_fusion = bf16[4096,512]{1,0:T(8,128)(2,1)} fusion(bf16[5120,512]{1,0:T(8,128)(2,1)} %get-tuple-element.187, s32[4096]{0:T(1024)S(1)} %fusion.37), kind=kCustom, calls=%fused_computation.clone.clone.1 | custom fusion | bytes 8404992 | tf_op jit(solution)/shard_map/while/body/eval_jaxpr/gather | solution.py:87
  219.7 7.0 fusion.38
  226.7 18.1 %scatter_fusion = f32[24,512,128]{2,1,0:T(8,128)} fusion(f32[24,512,128]{2,1,0:T(8,128)} %get-tuple-element.176, s32[32]{0:T(128)S(1)} %get-tuple-element.165, f32[32,512,128]{2,1,0:T(8,128)} %fusion.38), kind=kCustom, calls=%fused_computation.2.clone.clone.1 | custom fusion | flops 2097152 | bytes 25165952 | tf_op jit(solution)/shard_map/while/body/eval_jaxpr/scatter-add | solution.py:97
  244.9 20.6 %gather_fusion.1 = bf16[4096,512]{1,0:T(8,128)(2,1)} fusion(bf16[5120,512]{1,0:T(8,128)(2,1)} %get-tuple-element.189, s32[4096]{0:T(1024)S(1)} %fusion.37), kind=kCustom, calls=%fused_computation.1.clone.clone.1 | custom fusion | bytes 8404992 | tf_op jit(solution)/shard_map/while/body/eval_jaxpr/gather | solution.py:88
  265.5 7.0 fusion.39
  272.5 18.2 %scatter_fusion.1 = f32[24,128,512]{2,1,0:T(8,128)} fusion(f32[24,128,512]{2,1,0:T(8,128)} %get-tuple-element.177, s32[32]{0:T(128)S(1)} %get-tuple-element.165, f32[32,128,512]{2,1,0:T(8,128)} %fusion.39), kind=kCustom, calls=%fused_computation.3.clone.clone.1 | custom fusion | flops 2097152 | bytes 25165952 | tf_op jit(solution)/shard_map/while/body/eval_jaxpr/scatter-add | solution.py:97
  290.7 20.6 %gather_fusion = bf16[4096,512]{1,0:T(8,128)(2,1)} fusion(bf16[5120,512]{1,0:T(8,128)(2,1)} %get-tuple-element.187, s32[4096]{0:T(1024)S(1)} %fusion.37), kind=kCustom, calls=%fused_computation.clone.clone.1 | custom fusion | bytes 8404992 | tf_op jit(solution)/shard_map/while/body/eval_jaxpr/gather | solution.py:87
  311.4 7.0 fusion.38
  318.4 18.0 %scatter_fusion = f32[24,512,128]{2,1,0:T(8,128)} fusion(f32[24,512,128]{2,1,0:T(8,128)} %get-tuple-element.176, s32[32]{0:T(128)S(1)} %get-tuple-element.165, f32[32,512,128]{2,1,0:T(8,128)} %fusion.38), kind=kCustom, calls=%fused_computation.2.clone.clone.1 | custom fusion | flops 2097152 | bytes 25165952 | tf_op jit(solution)/shard_map/while/body/eval_jaxpr/scatter-add | solution.py:97
  336.5 20.6 %gather_fusion.1 = bf16[4096,512]{1,0:T(8,128)(2,1)} fusion(bf16[5120,512]{1,0:T(8,128)(2,1)} %get-tuple-element.189, s32[4096]{0:T(1024)S(1)} %fusion.37), kind=kCustom, calls=%fused_computation.1.clone.clone.1 | custom fusion | bytes 8404992 | tf_op jit(solution)/shard_map/while/body/eval_jaxpr/gather | solution.py:88
  357.2 7.0 fusion.39
  364.2 18.4 %scatter_fusion.1 = f32[24,128,512]{2,1,0:T(8,128)} fusion(f32[24,128,512]{2,1,0:T(8,128)} %get-tuple-element.177, s32[32]{0:T(128)S(1)} %get-tuple-element.165, f32[32,128,512]{2,1,0:T(8,128)} %fusion.39), kind=kCustom, calls=%fused_computation.3.clone.clone.1 | custom fusion | flops 2097152 | bytes 25165952 | tf_op jit(solution)/shard_map/while/body/eval_jaxpr/scatter-add | solution.py:97
  382.5 20.6 %gather_fusion = bf16[4096,512]{1,0:T(8,128)(2,1)} fusion(bf16[5120,512]{1,0:T(8,128)(2,1)} %get-tuple-element.187, s32[4096]{0:T(1024)S(1)} %fusion.37), kind=kCustom, calls=%fused_computation.clone.clone.1 | custom fusion | bytes 8404992 | tf_op jit(solution)/shard_map/while/body/eval_jaxpr/gather | solution.py:87
  403.2 7.0 fusion.38
  410.2 18.3 %scatter_fusion = f32[24,512,128]{2,1,0:T(8,128)} fusion(f32[24,512,128]{2,1,0:T(8,128)} %get-tuple-element.176, s32[32]{0:T(128)S(1)} %get-tuple-element.165, f32[32,512,128]{2,1,0:T(8,128)} %fusion.38), kind=kCustom, calls=%fused_computation.2.clone.clone.1 | custom fusion | flops 2097152 | bytes 25165952 | tf_op jit(solution)/shard_map/while/body/eval_jaxpr/scatter-add | solution.py:97
  428.6 20.6 %gather_fusion.1 = bf16[4096,512]{1,0:T(8,128)(2,1)} fusion(bf16[5120,512]{1,0:T(8,128)(2,1)} %get-tuple-element.189, s32[4096]{0:T(1024)S(1)} %fusion.37), kind=kCustom, calls=%fused_computation.1.clone.clone.1 | custom fusion | bytes 8404992 | tf_op jit(solution)/shard_map/while/body/eval_jaxpr/gather | solution.py:88
  449.3 7.0 fusion.39
  456.2 18.2 %scatter_fusion.1 = f32[24,128,512]{2,1,0:T(8,128)} fusion(f32[24,128,512]{2,1,0:T(8,128)} %get-tuple-element.177, s32[32]{0:T(128)S(1)} %get-tuple-element.165, f32[32,128,512]{2,1,0:T(8,128)} %fusion.39), kind=kCustom, calls=%fused_computation.3.clone.clone.1 | custom fusion | flops 2097152 | bytes 25165952 | tf_op jit(solution)/shard_map/while/body/eval_jaxpr/scatter-add | solution.py:97
  474.4 20.6 %gather_fusion = bf16[4096,512]{1,0:T(8,128)(2,1)} fusion(bf16[5120,512]{1,0:T(8,128)(2,1)} %get-tuple-element.187, s32[4096]{0:T(1024)S(1)} %fusion.37), kind=kCustom, calls=%fused_computation.clone.clone.1 | custom fusion | bytes 8404992 | tf_op jit(solution)/shard_map/while/body/eval_jaxpr/gather | solution.py:87
  495.1 7.0 fusion.38
  502.1 18.1 %scatter_fusion = f32[24,512,128]{2,1,0:T(8,128)} fusion(f32[24,512,128]{2,1,0:T(8,128)} %get-tuple-element.176, s32[32]{0:T(128)S(1)} %get-tuple-element.165, f32[32,512,128]{2,1,0:T(8,128)} %fusion.38), kind=kCustom, calls=%fused_computation.2.clone.clone.1 | custom fusion | flops 2097152 | bytes 25165952 | tf_op jit(solution)/shard_map/while/body/eval_jaxpr/scatter-add | solution.py:97
  520.3 0.7 reduce-scatter.3.cloned.1.call-update
  521.0 65.9 %reduce-scatter.5.cloned.1.call-done = f32[24,128,128]{2,1,0:T(8,128)} async-done(((f32[24,128,512]{2,1,0:T(8,128)}), f32[24,128,128]{2,1,0:T(8,128)}) %reduce-scatter.5.cloned.1.call-update) | async-done | bytes 1572880 | tf_op jit(solution)/shard_map/reduce_scatter | solution.py:108
  586.9 2.7 copy.29
  589.6 7.8 all-to-all-start.3
  597.5 58.3 %reduce-scatter.3.cloned.1.call-done = f32[24,128,128]{2,1,0:T(8,128)} async-done(((f32[24,512,128]{2,1,0:T(8,128)}), f32[24,128,128]{2,1,0:T(8,128)}) %reduce-scatter.3.cloned.1.call-update) | async-done | bytes 1572880 | tf_op jit(solution)/shard_map/reduce_scatter | solution.py:107
  655.8 3.5 copy.28
  659.2 7.6 all-to-all-start.2
  667.1 1.8 collective-permute-start.1
  668.9 2.1 collective-permute-start.2
  671.0 1.2 collective-permute-start.3
  672.4 2.8 collective-permute-start.5
  675.2 2.1 collective-permute-start.6
  677.3 2.8 collective-permute-start.7
  680.3 4.4 collective-permute-start.9
  684.8 1.9 collective-permute-start.10
  686.7 2.6 collective-permute-start.11
  689.4 4.1 collective-permute-start.13
  693.6 2.1 collective-permute-start.14
  695.8 1.5 collective-permute-done.13
  697.4 4.7 collective-permute-done.14
  702.1 0.3 copy.40
  702.4 3.0 all-to-all-done.2
  705.3 2.4 fusion.16
  707.7 75.4 %psum.7 = f32[24,24]{1,0:T(8,128)} all-reduce(f32[24,24]{1,0:T(8,128)S(1)} %fusion.16), channel_id=1, replica_groups=mesh['row'=4,'col'=16,'layer'=4] {'row','col','layer'}, use_global_device_ids=true, to_apply=%region_10.11 | all-reduce | flops 576 | bytes 4608 | tf_op jit(solution)/shard_map/psum | solution.py:131
  (58 shorter events, 1.7 us)
Async XLA Ops:
  11.0 31.6 %all-to-all-start = ((s32[64,2,2]{1,2,0:T(2,128)}), s32[64,2,2]{1,2,0:T(2,128)S(1)}, u32[]{:S(2)}, u32[]{:S(2)}) async-start(s32[64,2,2]{1,2,0:T(2,128)} %copy.25), calls=%async_computation | async-start | bytes 131072 | tf_op jit(solution)/shard_map/all_to_all | solution.py:68
  42.5 103.9 %all-to-all-start.1 = ((bf16[128,128,128]{2,1,0:T(8,128)(2,1)}), bf16[128,128,128]{2,1,0:T(8,128)(2,1)}, u32[]{:S(2)}, u32[]{:S(2)}) async-start(bf16[128,128,128]{2,1,0:T(8,128)(2,1)} %scatter_fusion.2), calls=%async_computation.1 | async-start | bytes 8388608 | tf_op jit(solution)/shard_map/all_to_all | solution.py:61
  53.0 534.0 %reduce-scatter.5.cloned.1.call-start = ((), (), s32[]{:S(2)}) async-start(), calls=%async_computation.7 | async-start | bytes 7864320 | tf_op jit(solution)/shard_map/reduce_scatter | solution.py:108
  520.3 135.5 %reduce-scatter.3.cloned.1.call-start = ((), (), s32[]{:S(2)}) async-start(), calls=%async_computation.6 | async-start | bytes 7864320 | tf_op jit(solution)/shard_map/reduce_scatter | solution.py:107
  589.6 69.6 %all-to-all-start.3 = ((f32[24,1,16,8,128]{4,3,0,1,2:T(8,128)}), f32[24,1,16,8,128]{4,3,0,1,2:T(8,128)S(1)}, u32[]{:S(2)}, u32[]{:S(2)}) async-start(f32[24,1,16,8,128]{4,3,0,1,2:T(8,128)} %copy.29), calls=%async_computation.5 | async-start | bytes 3145728 | tf_op jit(solution)/shard_map/all_to_all | solution.py:118
  659.2 46.1 %all-to-all-start.2 = ((f32[24,1,16,8,128]{4,0,3,1,2:T(8,128)}), f32[24,1,16,8,128]{4,0,3,1,2:T(8,128)S(1)}, u32[]{:S(2)}, u32[]{:S(2)}) async-start(f32[24,1,16,8,128]{4,0,3,1,2:T(8,128)} %bitcast.4), calls=%async_computation.3 | async-start | bytes 3145728 | tf_op jit(solution)/shard_map/all_to_all | solution.py:117
  667.0 5.4 collective-permute-start
  667.1 8.1 %collective-permute-start.1 = (f32[24,1,8,128]{3,2,0,1:T(8,128)S(1)}, f32[24,1,8,128]{3,2,0,1:T(8,128)S(1)}, u32[]{:S(2)}, u32[]{:S(2)}) collective-permute-start(f32[24,1,8,128]{3,2,0,1:T(8,128)S(1)} %get-tuple-element.118), channel_id=1, source_target_pairs={{0,2},{1,3},{2,0},{3,1},{64,66},{65,67},{66,64},{67,65},{128,130},... | collective-permute-start | bytes 294920 | tf_op jit(solution)/shard_map/ppermute | solution.py:20
  668.9 8.4 %collective-permute-start.2 = (f32[24,1,8,128]{3,2,0,1:T(8,128)S(1)}, f32[24,1,8,128]{3,2,0,1:T(8,128)S(1)}, u32[]{:S(2)}, u32[]{:S(2)}) collective-permute-start(f32[24,1,8,128]{3,2,0,1:T(8,128)S(1)} %get-tuple-element.117), channel_id=1, source_target_pairs={{0,3},{1,2},{2,1},{3,0},{64,67},{65,66},{66,65},{67,64},{128,131},... | collective-permute-start | bytes 294920 | tf_op jit(solution)/shard_map/ppermute | solution.py:20
  671.0 9.2 %collective-permute-start.3 = (f32[24,1,8,128]{3,2,0,1:T(8,128)S(1)}, f32[24,1,8,128]{3,2,0,1:T(8,128)S(1)}, u32[]{:S(2)}, u32[]{:S(2)}) collective-permute-start(f32[24,1,8,128]{3,2,0,1:T(8,128)S(1)} %get-tuple-element.116), channel_id=1, source_target_pairs={{0,64},{1,65},{2,66},{3,67},{64,0},{65,1},{66,2},{67,3},{128,192},... | collective-permute-start | bytes 294920 | tf_op jit(solution)/shard_map/ppermute | solution.py:20
  672.2 8.1 %collective-permute-start.4 = (f32[24,1,8,128]{3,2,0,1:T(8,128)S(1)}, f32[24,1,8,128]{3,2,0,1:T(8,128)S(1)}, u32[]{:S(2)}, u32[]{:S(2)}) collective-permute-start(f32[24,1,8,128]{3,2,0,1:T(8,128)S(1)} %get-tuple-element.115), channel_id=1, source_target_pairs={{0,65},{1,64},{2,67},{3,66},{64,1},{65,0},{66,3},{67,2},{128,193},... | collective-permute-start | bytes 294920 | tf_op jit(solution)/shard_map/ppermute | solution.py:20
  672.4 12.4 %collective-permute-start.5 = (f32[24,1,8,128]{3,2,0,1:T(8,128)S(1)}, f32[24,1,8,128]{3,2,0,1:T(8,128)S(1)}, u32[]{:S(2)}, u32[]{:S(2)}) collective-permute-start(f32[24,1,8,128]{3,2,0,1:T(8,128)S(1)} %get-tuple-element.114), channel_id=1, source_target_pairs={{0,66},{1,67},{2,64},{3,65},{64,2},{65,3},{66,0},{67,1},{128,194},... | collective-permute-start | bytes 294920 | tf_op jit(solution)/shard_map/ppermute | solution.py:20
  675.2 11.5 %collective-permute-start.6 = (f32[24,1,8,128]{3,2,0,1:T(8,128)S(1)}, f32[24,1,8,128]{3,2,0,1:T(8,128)S(1)}, u32[]{:S(2)}, u32[]{:S(2)}) collective-permute-start(f32[24,1,8,128]{3,2,0,1:T(8,128)S(1)} %get-tuple-element.113), channel_id=1, source_target_pairs={{0,67},{1,66},{2,65},{3,64},{64,3},{65,2},{66,1},{67,0},{128,195},... | collective-permute-start | bytes 294920 | tf_op jit(solution)/shard_map/ppermute | solution.py:20
  677.3 12.0 %collective-permute-start.7 = (f32[24,1,8,128]{3,2,0,1:T(8,128)S(1)}, f32[24,1,8,128]{3,2,0,1:T(8,128)S(1)}, u32[]{:S(2)}, u32[]{:S(2)}) collective-permute-start(f32[24,1,8,128]{3,2,0,1:T(8,128)S(1)} %get-tuple-element.112), channel_id=1, source_target_pairs={{0,128},{1,129},{2,130},{3,131},{64,192},{65,193},{66,194},{67,195... | collective-permute-start | bytes 294920 | tf_op jit(solution)/shard_map/ppermute | solution.py:20
  680.2 9.3 %collective-permute-start.8 = (f32[24,1,8,128]{3,2,0,1:T(8,128)S(1)}, f32[24,1,8,128]{3,2,0,1:T(8,128)S(1)}, u32[]{:S(2)}, u32[]{:S(2)}) collective-permute-start(f32[24,1,8,128]{3,2,0,1:T(8,128)S(1)} %get-tuple-element.111), channel_id=1, source_target_pairs={{0,129},{1,128},{2,131},{3,130},{64,193},{65,192},{66,195},{67,194... | collective-permute-start | bytes 294920 | tf_op jit(solution)/shard_map/ppermute | solution.py:20
  680.3 13.3 %collective-permute-start.9 = (f32[24,1,8,128]{3,2,0,1:T(8,128)S(1)}, f32[24,1,8,128]{3,2,0,1:T(8,128)S(1)}, u32[]{:S(2)}, u32[]{:S(2)}) collective-permute-start(f32[24,1,8,128]{3,2,0,1:T(8,128)S(1)} %get-tuple-element.110), channel_id=1, source_target_pairs={{0,130},{1,131},{2,128},{3,129},{64,194},{65,195},{66,192},{67,193... | collective-permute-start | bytes 294920 | tf_op jit(solution)/shard_map/ppermute | solution.py:20
  684.8 11.0 %collective-permute-start.10 = (f32[24,1,8,128]{3,2,0,1:T(8,128)S(1)}, f32[24,1,8,128]{3,2,0,1:T(8,128)S(1)}, u32[]{:S(2)}, u32[]{:S(2)}) collective-permute-start(f32[24,1,8,128]{3,2,0,1:T(8,128)S(1)} %get-tuple-element.109), channel_id=1, source_target_pairs={{0,131},{1,130},{2,129},{3,128},{64,195},{65,194},{66,193},{67,192... | collective-permute-start | bytes 294920 | tf_op jit(solution)/shard_map/ppermute | solution.py:20
  686.7 9.1 %collective-permute-start.11 = (f32[24,1,8,128]{3,2,0,1:T(8,128)S(1)}, f32[24,1,8,128]{3,2,0,1:T(8,128)S(1)}, u32[]{:S(2)}, u32[]{:S(2)}) collective-permute-start(f32[24,1,8,128]{3,2,0,1:T(8,128)S(1)} %get-tuple-element.108), channel_id=1, source_target_pairs={{0,192},{1,193},{2,194},{3,195},{64,128},{65,129},{66,130},{67,131... | collective-permute-start | bytes 294920 | tf_op jit(solution)/shard_map/ppermute | solution.py:20
  689.3 6.5 collective-permute-start.12
  689.4 7.9 %collective-permute-start.13 = (f32[24,1,8,128]{3,2,0,1:T(8,128)S(1)}, f32[24,1,8,128]{3,2,0,1:T(8,128)S(1)}, u32[]{:S(2)}, u32[]{:S(2)}) collective-permute-start(f32[24,1,8,128]{3,2,0,1:T(8,128)S(1)} %get-tuple-element.106), channel_id=1, source_target_pairs={{0,194},{1,195},{2,192},{3,193},{64,130},{65,131},{66,128},{67,129... | collective-permute-start | bytes 294920 | tf_op jit(solution)/shard_map/ppermute | solution.py:20
  693.6 8.4 %collective-permute-start.14 = (f32[24,1,8,128]{3,2,0,1:T(8,128)S(1)}, f32[24,1,8,128]{3,2,0,1:T(8,128)S(1)}, u32[]{:S(2)}, u32[]{:S(2)}) collective-permute-start(f32[24,1,8,128]{3,2,0,1:T(8,128)S(1)} %get-tuple-element.105), channel_id=1, source_target_pairs={{0,195},{1,194},{2,193},{3,192},{64,131},{65,130},{66,129},{67,128... | collective-permute-start | bytes 294920 | tf_op jit(solution)/shard_map/ppermute | solution.py:20
Sparse Core Ops, SparseCore 0:
  520.4 66.4 reduce-scatter.4
  589.5 66.2 reduce-scatter.2
